TPU v7x, 32 devices: a whole 2x2x4 slice. The times are simulated.
32 devices in a mesh: dp: 8 (over y, x, core), mp: 4 (over z).
Axes of the slice: x: 2, y: 2, z: 4, core: 2. Of those that a mesh axis runs over, the one named last changes fastest.
Arguments:
- queries: bfloat16 [2048, 2048], P('dp', 'mp'), may hold values from -24 to 24
- context_grad: bfloat16 [2048, 2048], P('dp', 'mp'), may hold values from -6 to 6
- encoder_rows: bfloat16 [7168, 4096], P('dp'), may hold values from -60 to 60
- key_weight: bfloat16 [4096, 2048], P('dp', 'mp'), may hold values from -1 to 1
- value_weight: bfloat16 [4096, 2048], P('dp', 'mp'), may hold values from -0.09375 to 0.09375
- document_lengths: int32 [8, 4], P('dp'), may hold values from 1 to 128, 256 in all within a row
- block_bin: int32 [56], P('dp'), may hold values from 0 to 7, as said below
- block_document: int32 [56], P('dp'), may hold values from 0 to 3
Outputs:
- context: bfloat16 [2048, 2048], P('dp', 'mp')
- query_grad: bfloat16 [2048, 2048], P('dp', 'mp')
- encoder_grad: bfloat16 [7168, 4096], P('dp', 'mp')
- key_weight_grad: bfloat16 [4096, 2048], P('dp', 'mp')
- value_weight_grad: bfloat16 [4096, 2048], P('dp', 'mp')
Inputs may be any that keep to these rules, and one draw needn't show every extreme that they name: `block_bin`: each index of dp holds 7 encoder blocks and sends them to 7 different bins; one bin receives a block from every index of dp.
All inputs are finite; a program needn't handle non-finite values.
Results may differ from a plain program's by a relative error of at most 0.03.
The roundings to bfloat16 on the way count: a program that leaves them out, or rounds other values in their place, can miss the bound.
Values may be sent and summed in bfloat16 or wider, within the bound.
A program may use at most 128 MiB of HBM per device.

v0:
```python
import jax
import jax.numpy as jnp
from jax import lax
from jax.sharding import PartitionSpec as P

HD = 256
BLK = 128


masked_value = -1e30


def attend_weights(scores, live_mask):
    present = jnp.any(live_mask, axis=1)[None, :, None]
    blocked = jnp.where(live_mask[None], scores, masked_value)
    highest = jnp.max(blocked, axis=2, keepdims=True)
    highest = jnp.where(present, highest, 0.0)
    raised = jnp.exp(jnp.where(live_mask[None], scores - highest, masked_value))
    totals = jnp.maximum(jnp.sum(raised, axis=2, keepdims=True), 1.0)
    return raised / totals


def token_documents(lengths, token_count):
    doc_ends = jnp.cumsum(lengths)
    positions = jnp.arange(token_count, dtype=jnp.int32)
    return jnp.sum((doc_ends[None, :] <= positions[:, None]).astype(jnp.int32), axis=1)


def per_device(
    queries,
    context_grad,
    encoder_rows,
    key_weight,
    value_weight,
    document_lengths,
    block_bin,
    block_document,
):
    bin_count = lax.axis_size("dp")
    full_key, full_value = (
        lax.all_gather(key_weight, "dp", axis=0, tiled=True),
        lax.all_gather(value_weight, "dp", axis=0, tiled=True),
    )
    head_width = full_key.shape[1]
    head_count = head_width // HD
    block_rows = BLK
    blocks_here = block_bin.shape[0]
    both_weights = jnp.concatenate([full_key, full_value], axis=1)
    projected = jnp.dot(encoder_rows, both_weights, preferred_element_type=jnp.float32).astype(
        jnp.bfloat16
    )
    route_table = (block_bin[:, None] == jnp.arange(bin_count, dtype=jnp.int32)[None, :]).astype(
        jnp.bfloat16
    )
    flat_blocks = projected.reshape(blocks_here, block_rows * 2 * head_width)
    outbound = lax.dot_general(
        route_table, flat_blocks, (((0,), (0,)), ((), ())), preferred_element_type=jnp.float32
    )
    outbound = outbound.astype(jnp.bfloat16).reshape(bin_count, block_rows, 2 * head_width)
    slot_docs = (
        lax.dot_general(
            route_table.astype(jnp.float32),
            (block_document + 1).astype(jnp.float32),
            (((0,), (0,)), ((), ())),
        )
        - 1.0
    )
    tag_rows = jnp.broadcast_to(slot_docs[:, None], (bin_count, block_rows)).astype(jnp.bfloat16)
    arrived, arrived_tags = (
        lax.all_to_all(outbound, "dp", split_axis=0, concat_axis=0, tiled=True),
        lax.all_to_all(tag_rows, "dp", split_axis=0, concat_axis=0, tiled=True),
    )
    key_slots = arrived[:, :, :head_width].reshape(bin_count * block_rows, head_count, HD)
    value_slots = arrived[:, :, head_width:].reshape(bin_count * block_rows, head_count, HD)
    token_count = queries.shape[0]
    token_docs = token_documents(document_lengths[0], token_count).astype(jnp.float32)
    live_mask = arrived_tags.reshape(-1).astype(jnp.float32)[None, :] == token_docs[:, None]
    query_heads = queries.reshape(token_count, head_count, HD)
    grad_heads = context_grad.reshape(token_count, head_count, HD)
    scaling = HD ** (-0.5)
    scores = (
        jnp.einsum("thd,shd->hts", query_heads, key_slots, preferred_element_type=jnp.float32)
        * scaling
    )
    attention = attend_weights(scores, live_mask)
    rounded = attention.astype(jnp.bfloat16)
    context = jnp.einsum(
        "hts,shd->thd", rounded, value_slots, preferred_element_type=jnp.float32
    ).astype(jnp.bfloat16)
    grad_raw = jnp.einsum(
        "thd,shd->hts", grad_heads, value_slots, preferred_element_type=jnp.float32
    )
    deltas = jnp.sum(attention * grad_raw, axis=2, keepdims=True)
    score_grad = (attention * (grad_raw - deltas) * scaling).astype(jnp.bfloat16)
    query_grad = jnp.einsum(
        "hts,shd->thd", score_grad, key_slots, preferred_element_type=jnp.float32
    ).astype(jnp.bfloat16)
    key_grad = jnp.einsum(
        "hts,thd->shd", score_grad, query_heads, preferred_element_type=jnp.float32
    ).astype(jnp.bfloat16)
    value_grad = jnp.einsum(
        "hts,thd->shd", rounded, grad_heads, preferred_element_type=jnp.float32
    ).astype(jnp.bfloat16)
    slot_grads = jnp.concatenate(
        [
            key_grad.reshape(bin_count, block_rows, head_width),
            value_grad.reshape(bin_count, block_rows, head_width),
        ],
        axis=2,
    )
    returned = lax.all_to_all(slot_grads, "dp", split_axis=0, concat_axis=0, tiled=True)
    own_grads = jnp.dot(
        route_table,
        returned.reshape(bin_count, block_rows * 2 * head_width),
        preferred_element_type=jnp.float32,
    )
    own_grads = own_grads.astype(jnp.bfloat16).reshape(encoder_rows.shape[0], 2 * head_width)
    weight_terms = lax.dot_general(
        encoder_rows, own_grads, (((0,), (0,)), ((), ())), preferred_element_type=jnp.float32
    )
    weight_sums = lax.psum_scatter(
        weight_terms.astype(jnp.bfloat16), "dp", scatter_dimension=0, tiled=True
    ).astype(jnp.float32)
    key_weight_grad = weight_sums[:, :head_width].astype(jnp.bfloat16)
    value_weight_grad = weight_sums[:, head_width:].astype(jnp.bfloat16)
    row_terms = lax.dot_general(
        own_grads, both_weights, (((1,), (1,)), ((), ())), preferred_element_type=jnp.float32
    )
    encoder_grad = lax.psum_scatter(
        row_terms.astype(jnp.bfloat16), "mp", scatter_dimension=1, tiled=True
    )
    return (
        context.reshape(token_count, head_width),
        query_grad.reshape(token_count, head_width),
        encoder_grad,
        key_weight_grad,
        value_weight_grad,
    )


def solution(mesh):
    in_specs = (
        P("dp", "mp"),
        P("dp", "mp"),
        P("dp", None),
        P("dp", "mp"),
        P("dp", "mp"),
        P("dp", None),
        P("dp"),
        P("dp"),
    )
    out_specs = (P("dp", "mp"), P("dp", "mp"), P("dp", "mp"), P("dp", "mp"), P("dp", "mp"))
    return jax.shard_map(
        per_device, mesh=mesh, in_specs=in_specs, out_specs=out_specs, check_vma=False
    )
```

profile of v0, /device:TPU:10, one launch (start us, length us, event | category | flops | bytes accessed | tf_op | source)
XLA Modules:
  0.0 425.6 jit_solution(468431480410873868)
XLA Ops:
  7.2 0.7 all-gather.3.cloned.1.call-update
  7.9 0.7 all-gather.5.cloned.1.call-update
  8.6 0.9 fusion.12
  9.5 0.7 broadcast_in_dim.30
  10.2 4.3 all-to-all-start.1
  14.4 33.2 %all-gather.3.cloned.1.call-done = bf16[4096,512]{1,0:T(8,128)(2,1)} async-done(((bf16[512,512]{1,0:T(8,128)(2,1)}), bf16[4096,512]{1,0:T(8,128)(2,1)}) %all-gather.3.cloned.1.call-update) | async-done | bytes 4194320 | tf_op jit(solution)/shard_map/all_gather | solution.py:41
  47.6 4.5 %constant_dynamic-update-slice_fusion.1 = bf16[4096,1024]{1,0:T(8,128)(2,1)} fusion(bf16[4096,512]{1,0:T(8,128)(2,1)} %all-gather.3.cloned.1.call-done), kind=kLoop, calls=%fused_computation.43 | loop fusion | bytes 8388608
  52.1 34.0 %all-gather.5.cloned.1.call-done = bf16[4096,512]{1,0:T(8,128)(2,1)} async-done(((bf16[512,512]{1,0:T(8,128)(2,1)}), bf16[4096,512]{1,0:T(8,128)(2,1)}) %all-gather.5.cloned.1.call-update) | async-done | bytes 4194320 | tf_op jit(solution)/shard_map/all_gather | solution.py:42
  86.1 4.5 %constant_dynamic-update-slice_fusion = bf16[4096,1024]{1,0:T(8,128)(2,1)} fusion(bf16[4096,1024]{1,0:T(8,128)(2,1)} %constant_dynamic-update-slice_fusion.1, bf16[4096,512]{1,0:T(8,128)(2,1)} %all-gather.5.cloned.1.call-done), kind=kLoop, calls=%fused_computation.42 | loop fusion | bytes 8388608 | tf_op jit(solution)/shard_map/concatenate | solution.py:48
  90.6 13.4 %convert_bitcast_fusion.1 = bf16[896,1024]{0,1:T(8,128)(2,1)S(1)} fusion(bf16[4096,1024]{1,0:T(8,128)(2,1)} %constant_dynamic-update-slice_fusion, bf16[896,4096]{1,0:T(8,128)(2,1)} %param.10), kind=kOutput, calls=%fused_computation.16 | convolution fusion | flops 7517110272 | bytes 17563648 | tf_op jit(solution)/shard_map/dot_general | solution.py:49
  104.0 2.4 copy.79
  106.4 3.8 reshape.137
  110.2 2.2 convolution_convert_fusion.1
  112.5 4.1 copy.80
  116.6 4.2 all-to-all-start
  121.3 24.6 %all-to-all-done = bf16[8,128,1024]{1,2,0:T(8,128)(2,1)S(1)} async-done(((bf16[8,128,1024]{1,2,0:T(8,128)(2,1)}), bf16[8,128,1024]{1,2,0:T(8,128)(2,1)S(1)}, u32[]{:S(2)}, u32[]{:S(2)}) %all-to-all-start) | async-done | bytes 2097184 | tf_op jit(solution)/shard_map/all_to_all | solution.py:70
  145.9 1.1 fusion.43
  147.0 0.7 copy.81
  147.7 0.5 reshape.139
  148.2 0.7 copy.82
  148.9 0.5 reshape.142
  149.4 1.8 fusion.4
  151.2 0.5 fusion.8
  151.8 0.6 copy-done.5
  152.4 1.9 fusion.17
  154.3 0.7 fusion.10
  155.0 0.5 copy.92
  155.8 6.1 %fusion.9 = bf16[1024,2,256]{2,0,1:T(8,128)(2,1)} fusion(f32[2,1024,256]{2,1,0:T(8,128)} %fusion.17, bf16[32,2,8,256]{3,2,1,0:T(8,128)(2,1)} %bitcast.136, f32[2,1024,256]{2,1,0:T(8,128)} %copy-done.1, f32[2,256]{1,0:T(2,128)S(1)} %broadcast_maximum_fusion, f32[2,256]{1,0:T(2,128)S(1)} %broadcast_select_fusion, pred[256,1024]{0,1:T(8,128)(4,1)S(1)} %get-tuple-element.35), kind=kOutput, calls=%fused_computation.21 | convolution fusion | flops 275777024 | bytes 5771264 | tf_op jit(solution)/shard_map/hts,thd->shd/dot_general | solution.py:98
  161.9 1.5 copy.90
  164.2 29.1 %all_to_all.16 = bf16[8,128,1024]{1,2,0:T(8,128)(2,1)S(1)} all-to-all(bf16[8,128,1024]{1,2,0:T(8,128)(2,1)S(1)} %copy.93), channel_id=1, replica_groups=mesh['dp'=8,'mp'=4] {'dp'}, dimensions={0} | all-to-all | bytes 4194304 | tf_op jit(solution)/shard_map/all_to_all | solution.py:111
  193.2 2.6 copy.94
  195.8 2.7 copy.107
  198.6 0.8 convolution_convert_fusion
  199.4 4.0 reshape.150
  203.3 13.8 %convert_bitcast_fusion = bf16[4096,1024]{0,1:T(8,128)(2,1)} fusion(bf16[896,1024]{1,0:T(8,128)(2,1)} %reshape.150, bf16[896,4096]{1,0:T(8,128)(2,1)} %param.10), kind=kOutput, calls=%fused_computation.3 | convolution fusion | flops 7520387072 | bytes 17563648 | tf_op jit(solution)/shard_map/dot_general | solution.py:118
  217.1 0.3 reduce-scatter.3.cloned.1.call-start
  217.4 1.2 copy-done.3
  218.6 13.2 %convolution_convert_fusion.2 = bf16[896,4096]{1,0:T(8,128)(2,1)} fusion(bf16[896,1024]{1,0:T(8,128)(2,1)S(1)} %copy-done.3, bf16[4096,1024]{1,0:T(8,128)(2,1)} %constant_dynamic-update-slice_fusion), kind=kOutput, calls=%fused_computation.4 | convolution fusion | flops 7519862784 | bytes 17563648 | tf_op jit(solution)/shard_map/dot_general | solution.py:126
  231.8 1.9 copy-done.2
  233.7 1.5 convolution_convert_fusion.6
  235.1 1.8 copy.95
  236.9 4.2 convolution_convert_fusion.5
  241.1 0.8 copy.96
  242.0 46.6 %reduce-scatter.5.cloned.1.call-done = bf16[512,1024]{0,1:T(8,128)(2,1)} async-done(((bf16[4096,1024]{0,1:T(8,128)(2,1)}), bf16[512,1024]{0,1:T(8,128)(2,1)}) %reduce-scatter.5.cloned.1.call-update) | async-done | bytes 1048592 | tf_op jit(solution)/shard_map/reduce_scatter | solution.py:121
  288.6 1.3 fusion.44
  289.8 1.0 copy.97
  290.8 1.0 copy.98
  291.8 127.3 %reduce-scatter.3.cloned.1.call-done = bf16[896,1024]{1,0:T(8,128)(2,1)} async-done(((bf16[896,4096]{1,0:T(8,128)(2,1)}), bf16[896,1024]{1,0:T(8,128)(2,1)}) %reduce-scatter.3.cloned.1.call-update) | async-done | bytes 1835024 | tf_op jit(solution)/shard_map/reduce_scatter | solution.py:129
  (30 shorter events, 1.7 us)
Async XLA Ops:
  7.2 40.4 %all-gather.3.cloned.1.call-start = ((), (), s32[]{:S(2)}) async-start(), calls=%async_computation.5 | async-start | bytes 4718592 | tf_op jit(solution)/shard_map/all_gather | solution.py:41
  7.9 78.2 %all-gather.5.cloned.1.call-start = ((), (), s32[]{:S(2)}) async-start(), calls=%async_computation.6 | async-start | bytes 4718592 | tf_op jit(solution)/shard_map/all_gather | solution.py:42
  10.2 106.4 %all-to-all-start.1 = ((bf16[8,1,128]{2,1,0:T(2,128)(2,1)}), bf16[8,1,128]{2,1,0:T(2,128)(2,1)S(1)}, u32[]{:S(2)}, u32[]{:S(2)}) async-start(bf16[8,1,128]{2,1,0:T(2,128)(2,1)} %broadcast_in_dim.30), calls=%async_computation.1 | async-start | bytes 8192 | tf_op jit(solution)/shard_map/all_to_all | solution.py:71
  106.4 3.8 copy-start.6
  116.6 4.2 copy-start.7
  116.6 29.3 %all-to-all-start = ((bf16[8,128,1024]{1,2,0:T(8,128)(2,1)}), bf16[8,128,1024]{1,2,0:T(8,128)(2,1)S(1)}, u32[]{:S(2)}, u32[]{:S(2)}) async-start(bf16[8,128,1024]{1,2,0:T(8,128)(2,1)} %copy.80), calls=%async_computation | async-start | bytes 4194304 | tf_op jit(solution)/shard_map/all_to_all | solution.py:70
  120.8 167.8 %reduce-scatter.5.cloned.1.call-start = ((), (), s32[]{:S(2)}) async-start(), calls=%async_computation.8 | async-start | bytes 9437184 | tf_op jit(solution)/shard_map/reduce_scatter | solution.py:121
  147.0 1.2 copy-start
  149.4 2.3 copy-start.4
  151.2 3.1 copy-start.1
  151.2 1.1 copy-start.5
  217.1 1.5 copy-start.3
  217.1 202.0 %reduce-scatter.3.cloned.1.call-start = ((), (), s32[]{:S(2)}) async-start(), calls=%async_computation.7 | async-start | bytes 9175040 | tf_op jit(solution)/shard_map/reduce_scatter | solution.py:129
  231.8 1.9 copy-start.2
Sparse Core Ops, SparseCore 0:
  9.9 37.7 all-gather.2
  49.5 36.5 all-gather.4
  217.2 71.2 reduce-scatter.4
  291.3 127.7 reduce-scatter.2
where the time goes:
time: 428 us; the launch traced here: 426 us
  waiting for transfers between devices  267 us (62%)
  matrix products  60.4 us (14%)
  local copies, waits for them, and re-layouts  45.1 us (11%)
  blocking collectives  29.1 us (7%)
  between operations  13.9 us (3%)
  starting transfers between devices  8.84 us (2%)
    reduce_scatter x1, waiting for transfers between devices, per_device(): lax.psum_scatter(row_terms.astype(jnp.bfloat16), 'mp', scatter_dimension=...  127 us
    reduce_scatter x1, waiting for transfers between devices, per_device(): lax.psum_scatter(weight_terms.astype(jnp.bfloat16), 'dp', scatter_dimensi...  46.6 us
    all_gather x1, waiting for transfers between devices, per_device(): lax.all_gather(value_weight, 'dp', axis=0, tiled=True)  34 us
    all_gather x1, waiting for transfers between devices, per_device(): lax.all_gather(key_weight, 'dp', axis=0, tiled=True)  33.2 us
    all_to_all x1, blocking collectives, per_device(): lax.all_to_all(slot_grads, 'dp', split_axis=0, concat_axis=0, tiled=True)  29.1 us
    all_to_all x1, waiting for transfers between devices, per_device(): lax.all_to_all(outbound, 'dp', split_axis=0, concat_axis=0, tiled=True)  24.6 us
    unnamed x24, local copies, waits for them, and re-layouts  16.1 us
    dot_general x1, matrix products, per_device(): lax.dot_general(encoder_rows, own_grads, (((0,), (0,)), ((), ())), prefer...  13.8 us
  transfers between devices with their start and end apart: 6, of which 5 were waited for; matrix products, arithmetic and copies ran while one was open for 15% of the time, Pallas kernels for 0%

commit v1 on v0

--- a/solution.py
+++ b/solution.py
@@ -1,6 +1,10 @@
+import functools
+
 import jax
 import jax.numpy as jnp
 from jax import lax
+from jax.experimental import pallas as pl
+from jax.experimental.pallas import tpu as pltpu
 from jax.sharding import PartitionSpec as P
 
 HD = 256
@@ -138,6 +142,414 @@
     )
 
 
+MESH = pl.DeviceIdType.MESH
+
+
+def contract(a, b, dim_a, dim_b):
+    return lax.dot_general(
+        a, b, (((dim_a,), (dim_b,)), ((), ())), preferred_element_type=jnp.float32
+    )
+
+
+def front_kernel(
+    n,
+    q_ref,
+    g_ref,
+    enc_hbm,
+    kw_ref,
+    vw_ref,
+    tags_ref,
+    routes_ref,
+    token_doc_ref,
+    ctx_ref,
+    qg_ref,
+    back_hbm,
+    wfull_hbm,
+    enc,
+    wts,
+    acc,
+    outbound,
+    arrived,
+    arrived_tags,
+    grads,
+    ret,
+    local_sem,
+    gather_send,
+    gather_recv,
+    tag_send,
+    tag_recv,
+    out_send,
+    out_recv,
+    back_send,
+    back_recv,
+):
+    me = lax.axis_index("dp")
+    core = me % 2
+    x = (me // 2) % 2
+    y = me // 4
+
+    def place(py, px, pc):
+        return (py * 2 + px) * 2 + pc
+
+    at_x, at_y = place(y, 1 - x, core), place(1 - y, x, core)
+    at_c, at_d = place(y, x, 1 - core), place(1 - y, 1 - x, core)
+    c_x, c_y = place(y, 1 - x, 1 - core), place(1 - y, x, 1 - core)
+    c_d = place(1 - y, 1 - x, 1 - core)
+    depth, width = kw_ref.shape
+    rows = enc.shape[0]
+    slots = n
+    blk = BLK
+
+    load_enc = pltpu.make_async_copy(enc_hbm, enc, local_sem.at[0])
+    load_enc.start()
+    barrier = pltpu.get_barrier_semaphore()
+    for d in range(1, n):
+        pl.semaphore_signal(
+            barrier, inc=1, device_id={"dp": (me + d) % n}, device_id_type=MESH
+        )
+    pl.semaphore_wait(barrier, n - 1)
+
+    def land(src, part):
+        return wts.at[src, :, pl.ds(part * width, width)]
+
+    started = []
+
+    def ship(ident, ref, src, part, to):
+        copy = pltpu.make_async_remote_copy(
+            src_ref=ref,
+            dst_ref=land(src, part),
+            send_sem=gather_send.at[ident],
+            recv_sem=gather_recv.at[ident],
+            device_id={"dp": to},
+            device_id_type=MESH,
+        )
+        copy.start()
+        started.append(copy)
+
+    def landed(ident, src, part):
+        pltpu.make_async_remote_copy(
+            src_ref=land(src, part),
+            dst_ref=land(src, part),
+            send_sem=gather_send.at[ident],
+            recv_sem=gather_recv.at[ident],
+            device_id={"dp": at_c},
+            device_id_type=MESH,
+        ).wait_recv()
+
+    ship(0, kw_ref, me, 0, at_x)
+    ship(3, vw_ref, me, 1, at_y)
+    ship(1, vw_ref, me, 1, at_x)
+    ship(2, kw_ref, me, 0, at_y)
+    ship(6, kw_ref, me, 0, at_c)
+    ship(7, vw_ref, me, 1, at_c)
+    own_k = pltpu.make_async_copy(kw_ref, land(me, 0), local_sem.at[1])
+    own_v = pltpu.make_async_copy(vw_ref, land(me, 1), local_sem.at[2])
+    own_k.start()
+    own_v.start()
+    tag_copies = []
+    for d in range(1, n):
+        to = (me + d) % n
+        copy = pltpu.make_async_remote_copy(
+            src_ref=tags_ref.at[to],
+            dst_ref=arrived_tags.at[me],
+            send_sem=tag_send.at[d],
+            recv_sem=tag_recv.at[d],
+            device_id={"dp": to},
+            device_id_type=MESH,
+        )
+        copy.start()
+        tag_copies.append(copy)
+    arrived_tags[me] = tags_ref[me]
+    own_k.wait()
+    own_v.wait()
+    load_enc.wait()
+
+    tile = rows // 2
+
+    def multiply(src, part, first=False):
+        columns = pl.ds(pl.multiple_of(src * depth, depth), depth)
+        cols = pl.ds(part * width, width)
+
+        @pl.loop(0, 2)
+        def _(t):
+            r = pl.ds(pl.multiple_of(t * tile, tile), tile)
+            product = jnp.dot(
+                enc[r, columns], wts[src, :, cols], preferred_element_type=jnp.float32
+            )
+            if first:
+                acc[r, cols] = product
+            else:
+                acc[r, cols] += product
+
+    multiply(me, 0, True)
+    multiply(me, 1, True)
+    landed(6, at_c, 0)
+    multiply(at_c, 0)
+    landed(7, at_c, 1)
+    multiply(at_c, 1)
+    landed(0, at_x, 0)
+    ship(4, land(at_x, 0), at_x, 0, at_y)
+    ship(8, land(at_x, 0), at_x, 0, at_c)
+    landed(3, at_y, 1)
+    ship(5, land(at_y, 1), at_y, 1, at_x)
+    ship(11, land(at_y, 1), at_y, 1, at_c)
+    multiply(at_x, 0)
+    multiply(at_y, 1)
+    landed(8, c_x, 0)
+    multiply(c_x, 0)
+    landed(11, c_y, 1)
+    multiply(c_y, 1)
+    landed(1, at_x, 1)
+    ship(9, land(at_x, 1), at_x, 1, at_c)
+    landed(2, at_y, 0)
+    ship(10, land(at_y, 0), at_y, 0, at_c)
+    multiply(at_x, 1)
+    multiply(at_y, 0)
+    landed(9, c_x, 1)
+    multiply(c_x, 1)
+    landed(10, c_y, 0)
+    multiply(c_y, 0)
+    landed(4, at_d, 0)
+    ship(12, land(at_d, 0), at_d, 0, at_c)
+    landed(5, at_d, 1)
+    ship(13, land(at_d, 1), at_d, 1, at_c)
+    multiply(at_d, 0)
+    multiply(at_d, 1)
+    landed(12, c_d, 0)
+    multiply(c_d, 0)
+    landed(13, c_d, 1)
+    multiply(c_d, 1)
+    keep = pltpu.make_async_copy(wts, wfull_hbm, local_sem.at[3])
+    keep.start()
+
+    out_copies = []
+    mine = pl.ds(pl.multiple_of(me * blk, blk), blk)
+    for d in [*range(1, n), 0]:
+        to = (me + d) % n
+
+        @pl.loop(0, blk // 16)
+        def _(t):
+            picked = jnp.zeros((16, 2 * width), jnp.float32)
+            for b in range(rows // blk):
+                row = routes_ref[to, b : b + 1, :]
+                wide = jnp.concatenate([row] * (2 * width // BLK), axis=1) > 0.5
+                part = acc[pl.ds(pl.multiple_of(b * blk + t * 16, 16), 16), :]
+                picked = jnp.where(wide, part, picked)
+            outbound[to, pl.ds(pl.multiple_of(t * 16, 16), 16), :] = picked.astype(jnp.bfloat16)
+
+        if d == 0:
+            arrived[mine, :] = outbound[to]
+            continue
+        copy = pltpu.make_async_remote_copy(
+            src_ref=outbound.at[to],
+            dst_ref=arrived.at[mine, :],
+            send_sem=out_send.at[d],
+            recv_sem=out_recv.at[d],
+            device_id={"dp": to},
+            device_id_type=MESH,
+        )
+        copy.start()
+        out_copies.append(copy)
+
+    token_doc = token_doc_ref[:, 0:1]
+    for copy in tag_copies:
+        copy.wait()
+    for copy in out_copies:
+        copy.wait()
+    tag_row = jnp.concatenate([arrived_tags[s, 0:1, :] for s in range(slots)], axis=1)
+    live = tag_row == token_doc
+    present = jnp.max(jnp.where(live, 1.0, 0.0), axis=1, keepdims=True) > 0.0
+    scaling = HD ** (-0.5)
+    back_copies = []
+    for h in range(width // HD):
+        hk, hv = pl.ds(h * HD, HD), pl.ds(width + h * HD, HD)
+        q, g = q_ref[:, hk], g_ref[:, hk]
+        scores = contract(q, arrived[:, hk], 1, 1) * scaling
+        highest = jnp.max(jnp.where(live, scores, masked_value), axis=1, keepdims=True)
+        highest = jnp.where(present, highest, 0.0)
+        raised = jnp.exp(jnp.where(live, scores - highest, masked_value))
+        totals = jnp.maximum(jnp.sum(raised, axis=1, keepdims=True), 1.0)
+        attention = raised / totals
+        rounded = attention.astype(jnp.bfloat16)
+        grad_raw = contract(g, arrived[:, hv], 1, 1)
+        deltas = jnp.sum(attention * grad_raw, axis=1, keepdims=True)
+        score_grad = (attention * (grad_raw - deltas) * scaling).astype(jnp.bfloat16)
+        grads[h, 0] = contract(score_grad, q, 0, 0).astype(jnp.bfloat16)
+        grads[h, 1] = contract(rounded, g, 0, 0).astype(jnp.bfloat16)
+        for d in range(1, n):
+            to = (me + d) % n
+            copy = pltpu.make_async_remote_copy(
+                src_ref=grads.at[h, :, pl.ds(pl.multiple_of(to * blk, blk), blk), :],
+                dst_ref=ret.at[h, :, pl.ds(pl.multiple_of(me * blk, blk), blk), :],
+                send_sem=back_send.at[h, d],
+                recv_sem=back_recv.at[h, d],
+                device_id={"dp": to},
+                device_id_type=MESH,
+            )
+            copy.start()
+            back_copies.append(copy)
+        ret[h, :, mine, :] = grads[h, :, mine, :]
+        ctx_ref[:, hk] = jnp.dot(
+            rounded, arrived[:, hv], preferred_element_type=jnp.float32
+        ).astype(jnp.bfloat16)
+        qg_ref[:, hk] = jnp.dot(
+            score_grad, arrived[:, hk], preferred_element_type=jnp.float32
+        ).astype(jnp.bfloat16)
+    for copy in started:
+        copy.wait_send()
+    keep.wait()
+    for copy in back_copies:
+        copy.wait()
+    put = pltpu.make_async_copy(ret, back_hbm, local_sem.at[0])
+    put.start()
+    put.wait()
+
+
+def pick_kernel(bins_ref, back_ref, own_ref):
+    heads = back_ref.shape[0]
+    for h in range(heads):
+        own_ref[:, pl.ds(h * HD, HD)] = back_ref[h, 0]
+        own_ref[:, pl.ds((heads + h) * HD, HD)] = back_ref[h, 1]
+
+
+def pick_blocks(back, bins):
+    heads = back.shape[0]
+    count = bins.shape[0]
+    return pl.pallas_call(
+        pick_kernel,
+        out_shape=jax.ShapeDtypeStruct((count * BLK, 2 * heads * HD), back.dtype),
+        grid_spec=pltpu.PrefetchScalarGridSpec(
+            num_scalar_prefetch=1,
+            grid=(count,),
+            in_specs=[pl.BlockSpec((heads, 2, BLK, HD), lambda b, bins: (0, 0, bins[b], 0))],
+            out_specs=pl.BlockSpec((BLK, 2 * heads * HD), lambda b, bins: (b, 0)),
+        ),
+    )(bins, back)
+
+
+def front(n, queries, context_grad, encoder_rows, key_weight, value_weight, lengths, bins, docs):
+    rows, model = encoder_rows.shape
+    depth, width = key_weight.shape
+    heads = width // HD
+    tokens = queries.shape[0]
+    hits = bins[:, None] == jnp.arange(n, dtype=jnp.int32)[None, :]
+    slot_docs = jnp.sum(jnp.where(hits, docs[:, None] + 1, 0), axis=0) - 1
+    tags = jnp.broadcast_to(slot_docs.astype(jnp.float32)[:, None, None], (n, 8, BLK))
+    padded = jnp.pad(hits.astype(jnp.float32).T, ((0, 0), (0, -bins.shape[0] % 8)))
+    routes = jnp.broadcast_to(padded[:, :, None], (n, padded.shape[1], BLK))
+    position = lax.broadcasted_iota(jnp.int32, (tokens, BLK), 0)
+    token_doc = jnp.zeros((tokens, BLK), jnp.float32)
+    end = jnp.int32(0)
+    for k in range(lengths.shape[1]):
+        end = end + lengths[0, k]
+        token_doc = token_doc + jnp.where(position >= end, 1.0, 0.0)
+    vmem = pl.BlockSpec(memory_space=pltpu.VMEM)
+    hbm = pl.BlockSpec(memory_space=pl.ANY)
+    bf16 = jnp.bfloat16
+    dma = pltpu.SemaphoreType.DMA
+    return pl.pallas_call(
+        functools.partial(front_kernel, n),
+        out_shape=(
+            jax.ShapeDtypeStruct((tokens, width), bf16),
+            jax.ShapeDtypeStruct((tokens, width), bf16),
+            jax.ShapeDtypeStruct((heads, 2, n * BLK, HD), bf16),
+            jax.ShapeDtypeStruct((n, depth, 2 * width), bf16),
+        ),
+        in_specs=[vmem, vmem, hbm, vmem, vmem, vmem, vmem, vmem],
+        out_specs=(vmem, vmem, hbm, hbm),
+        scratch_shapes=[
+            pltpu.VMEM((rows, model), bf16),
+            pltpu.VMEM((n, depth, 2 * width), bf16),
+            pltpu.VMEM((rows, 2 * width), jnp.float32),
+            pltpu.VMEM((n, BLK, 2 * width), bf16),
+            pltpu.VMEM((n * BLK, 2 * width), bf16),
+            pltpu.VMEM((n, 8, BLK), jnp.float32),
+            pltpu.VMEM((heads, 2, n * BLK, HD), bf16),
+            pltpu.VMEM((heads, 2, n * BLK, HD), bf16),
+            dma((4,)),
+            dma((14,)),
+            dma((14,)),
+            dma((n,)),
+            dma((n,)),
+            dma((n,)),
+            dma((n,)),
+            dma((heads, n)),
+            dma((heads, n)),
+        ],
+        compiler_params=pltpu.CompilerParams(
+            collective_id=0, has_side_effects=True, vmem_limit_bytes=62 * 1024 * 1024
+        ),
+    )(
+        queries,
+        context_grad,
+        encoder_rows,
+        key_weight,
+        value_weight,
+        tags,
+        routes,
+        token_doc,
+    )
+
+
+def line_sum(part_of, count):
+    z = lax.axis_index("mp")
+    total = part_of(z)
+    for direction in (1, -1):
+        carried = None
+        for step in range(count - 1):
+            if direction == 1:
+                dest = jnp.clip(z + count - 1 - step, 0, count - 1)
+                pairs = [(k, k + 1) for k in range(count - 1) if k <= step]
+            else:
+                dest = jnp.clip(z - (count - 1) + step, 0, count - 1)
+                pairs = [(k, k - 1) for k in range(1, count) if count - 1 - k <= step]
+            term = part_of(dest)
+            if carried is not None:
+                term = term + carried.astype(jnp.float32)
+            carried = lax.ppermute(term.astype(jnp.bfloat16), "mp", pairs)
+        total = total + carried.astype(jnp.float32)
+    return total.astype(jnp.bfloat16)
+
+
+def per_device_cube(
+    queries,
+    context_grad,
+    encoder_rows,
+    key_weight,
+    value_weight,
+    document_lengths,
+    block_bin,
+    block_document,
+):
+    n, count = lax.axis_size("dp"), lax.axis_size("mp")
+    width = key_weight.shape[1]
+    context, query_grad, back, weights = front(
+        n,
+        queries,
+        context_grad,
+        encoder_rows,
+        key_weight,
+        value_weight,
+        document_lengths,
+        block_bin,
+        block_document,
+    )
+    weights = weights.reshape(-1, 2 * width)
+    own = pick_blocks(back, block_bin)
+    out_width = weights.shape[0] // count
+    weight_terms = contract(encoder_rows, own, 0, 0)
+    weight_sums = lax.psum_scatter(
+        weight_terms.astype(jnp.bfloat16), "dp", scatter_dimension=0, tiled=True
+    )
+
+    def part_of(dest):
+        piece = lax.dynamic_slice_in_dim(weights, dest * out_width, out_width, 0)
+        return contract(own, piece, 1, 1)
+
+    encoder_grad = line_sum(part_of, count)
+    return context, query_grad, encoder_grad, weight_sums[:, :width], weight_sums[:, width:]
+
+
 def solution(mesh):
     in_specs = (
         P("dp", "mp"),
@@ -150,6 +562,7 @@
         P("dp"),
     )
     out_specs = (P("dp", "mp"), P("dp", "mp"), P("dp", "mp"), P("dp", "mp"), P("dp", "mp"))
+    cube = mesh.shape["dp"] == 2 * 2 * 2
     return jax.shard_map(
-        per_device, mesh=mesh, in_specs=in_specs, out_specs=out_specs, check_vma=False
-    )
+        per_device_cube if cube else per_device, mesh=mesh, in_specs=in_specs, out_specs=out_specs, check_vma=False
+    )

time: 428 us -> 302 us (0.71)
  waiting for transfers between devices: 267 us -> 105 us
  Pallas kernels: 0 us -> 99.4 us
  local copies, waits for them, and re-layouts: 45.1 us -> 9.75 us
  blocking collectives: 29.1 us -> 0 us
  matrix products: 60.4 us -> 47.8 us
  other arithmetic: 1.23 us -> 11.2 us
    reduce_scatter x2 -> x1, waiting for transfers between devices: 174 us -> 0.01 us  [per_device_cube(): lax.psum_scatter(weight_terms.astype(jnp.bfloat16), 'dp', scatter_dimensi...]
    ppermute x0 -> x6, waiting for transfers between devices: none -> 105 us  [line_sum(): carried = lax.ppermute(term.astype(jnp.bfloat16), 'mp', pairs)]
    pallas_call x0 -> x2, Pallas kernels: none -> 99.4 us  [the longest x1 93.6 us: front(): pl.pallas_call(functools.partial(front_kernel, n), out_shape=(jax.ShapeDt...]
    all_gather x2 -> x0, waiting for transfers between devices: 67.2 us -> none  [the longest x1 34 us: per_device(): lax.all_gather(value_weight, 'dp', axis=0, tiled=True)]
    all_to_all x1 -> x0, blocking collectives: 29.1 us -> none  [per_device(): lax.all_to_all(slot_grads, 'dp', split_axis=0, concat_axis=0, tiled=True)]
    all_to_all x2 -> x0, waiting for transfers between devices: 24.6 us -> none  [the longest x1 24.6 us: per_device(): lax.all_to_all(outbound, 'dp', split_axis=0, concat_axis=0, tiled=True)]
    reshape x5 -> x0, local copies, waits for them, and re-layouts: 12.9 us -> none  [the longest x1 4.11 us: per_device(): outbound.astype(jnp.bfloat16).reshape(bin_count, block_rows, 2 * head_width)]
    dot_general x12 -> x8, matrix products: 60.4 us -> 47.8 us  [contract(): lax.dot_general(a, b, (((dim_a,), (dim_b,)), ((), ())), preferred_element...]
  transfers between devices with their start and end apart: 6 -> 7, of which waited for: 5 -> 5; matrix products, arithmetic and copies ran while one was open for 15% -> 14% of each run, Pallas kernels for 0% -> 0%
where the time goes in v1:
time: 302 us; the launch traced here: 300 us
  waiting for transfers between devices  105 us (35%)
  Pallas kernels  99.4 us (33%)
  matrix products  47.8 us (16%)
  between operations  16.8 us (6%)
  other arithmetic  11.2 us (4%)
  starting transfers between devices  10.5 us (3%)
  local copies, waits for them, and re-layouts  9.75 us (3%)
    ppermute x6, waiting for transfers between devices, line_sum(): carried = lax.ppermute(term.astype(jnp.bfloat16), 'mp', pairs)  105 us
    pallas_call x1, Pallas kernels, front(): pl.pallas_call(functools.partial(front_kernel, n), out_shape=(jax.ShapeDt...  93.6 us
    dot_general x8, matrix products, contract(): lax.dot_general(a, b, (((dim_a,), (dim_b,)), ((), ())), preferred_element...  47.8 us
    ppermute x6, starting transfers between devices, line_sum(): carried = lax.ppermute(term.astype(jnp.bfloat16), 'mp', pairs)  10.4 us
  transfers between devices with their start and end apart: 7, of which 5 were waited for; matrix products, arithmetic and copies ran while one was open for 14% of the time, Pallas kernels for 0%

profile of v1, /device:TPU:10, one launch (start us, length us, event | category | flops | bytes accessed | tf_op | source)
XLA Modules:
  0.0 300.2 jit_solution(13438286217180157910)
XLA Ops:
  7.2 0.0 reduce-scatter.2.cloned.1.call-start
  7.2 1.4 fusion.35
  11.2 0.7 fusion.33
  11.9 0.7 iota_compare_fusion
  12.5 0.7 broadcast_add_fusion
  13.2 0.7 select_reduce_fusion
  13.9 0.8 iota.21.token_doc_ref
  14.7 0.7 broadcast_in_dim.44.routes_ref
  15.4 0.7 broadcast_in_dim.43.tags_ref
  16.1 93.6 %shard_map.119 = (bf16[256,512]{1,0:T(8,128)(2,1)}, bf16[256,512]{1,0:T(8,128)(2,1)}, bf16[2,2,1024,256]{3,2,1,0:T(8,128)(2,1)}, bf16[8,512,1024]{2,1,0:T(8,128)(2,1)}) custom-call(bf16[256,512]{1,0:T(8,128)(2,1)} %q_ref.1, bf16[256,512]{1,0:T(8,128)(2,1)} %g_ref.1, bf16[896,4096]{1,0:T(8,128)(2,1)} %enc_hbm.1, bf16[512,512]{1,0:T(8,128)(2,1)} %kw_ref.1, ...), custom_call_target="tpu_custom_call" | custom-call | tf_op jit(solution)/shard_map/pallas_call | solution.py:450
  109.7 5.8 %shard_map.120 = bf16[896,1024]{1,0:T(8,128)(2,1)} custom-call(s32[7]{0:T(128)} %bins_ref.1, bf16[2,2,1024,256]{3,2,1,0:T(8,128)(2,1)} %get-tuple-element.11.back_ref), custom_call_target="tpu_custom_call" | custom-call | tf_op jit(solution)/shard_map/pallas_call | solution.py:418
  115.5 13.7 %convert_bitcast_fusion = bf16[4096,1024]{0,1:T(8,128)(2,1)} fusion(bf16[896,1024]{1,0:T(8,128)(2,1)} %shard_map.120, bf16[896,4096]{1,0:T(8,128)(2,1)} %enc_hbm.1), kind=kOutput, calls=%fused_computation | convolution fusion | flops 7520387072 | bytes 17563648 | tf_op jit(solution)/shard_map/dot_general | solution.py:149
  129.2 0.0 copy-start
  129.2 0.0 reduce-scatter.2.cloned.1.call-update
  129.2 1.5 copy-done
  130.7 5.0 %fusion.14 = bf16[896,1024]{1,0:T(8,128)(2,1)} fusion(bf16[896,1024]{1,0:T(8,128)(2,1)S(1)} %copy-done, bf16[4096,1024]{1,0:T(8,128)(2,1)} %bitcast.16, s32[]{:T(128)S(6)} %select_n.50), kind=kOutput, calls=%fused_computation.20 | convolution fusion | flops 1879965696 | bytes 5767172 | tf_op jit(solution)/shard_map/dot_general | solution.py:149
  135.7 1.3 collective-permute-start
  137.0 5.2 %fusion.17 = bf16[896,1024]{1,0:T(8,128)(2,1)} fusion(bf16[896,1024]{1,0:T(8,128)(2,1)S(1)} %copy-done, bf16[4096,1024]{1,0:T(8,128)(2,1)} %bitcast.17, s32[]{:T(128)S(6)} %select_n.53), kind=kOutput, calls=%fused_computation.21 | convolution fusion | flops 1879965696 | bytes 5767172 | tf_op jit(solution)/shard_map/dot_general | solution.py:149
  142.2 1.9 collective-permute-start.3
  144.1 0.0 copy-start.1
  144.1 35.3 %collective-permute-done = bf16[896,1024]{1,0:T(8,128)(2,1)} collective-permute-done((bf16[896,1024]{1,0:T(8,128)(2,1)}, bf16[896,1024]{1,0:T(8,128)(2,1)}, u32[]{:S(2)}, u32[]{:S(2)}) %collective-permute-start) | collective-permute-done | bytes 1835040 | tf_op jit(solution)/shard_map/ppermute | solution.py:509
  179.4 5.6 %add_convert_fusion.4 = bf16[896,1024]{1,0:T(8,128)(2,1)} fusion(bf16[896,1024]{1,0:T(8,128)(2,1)} %collective-permute-done, bf16[896,1024]{1,0:T(8,128)(2,1)S(1)} %copy-done, bf16[4096,1024]{1,0:T(8,128)(2,1)} %bitcast.18, s32[]{:T(128)S(6)} %select_n.49), kind=kOutput, calls=%fused_computation.5 | convolution fusion | flops 1881800704 | bytes 7602180 | tf_op jit(solution)/shard_map/dot_general | solution.py:149
  185.0 1.9 collective-permute-start.1
  186.9 0.0 collective-permute-done.3
  186.9 0.0 copy-done.1
  186.9 6.0 %add_convert_fusion.2 = bf16[896,1024]{1,0:T(8,128)(2,1)} fusion(bf16[896,1024]{1,0:T(8,128)(2,1)} %collective-permute-done.3, bf16[896,1024]{1,0:T(8,128)(2,1)S(1)} %copy-done.1, bf16[4096,1024]{1,0:T(8,128)(2,1)} %bitcast.19, s32[]{:T(128)S(6)} %select_n.52), kind=kOutput, calls=%fused_computation.3 | convolution fusion | flops 1881800704 | bytes 7602180 | tf_op jit(solution)/shard_map/dot_general | solution.py:149
  192.9 1.3 collective-permute-start.4
  194.2 0.0 copy-start.2
  194.2 4.4 %fusion.10 = f32[896,1024]{1,0:T(8,128)S(1)} fusion(bf16[896,1024]{1,0:T(8,128)(2,1)} %shard_map.120, bf16[4096,1024]{1,0:T(8,128)(2,1)} %bitcast.20, s32[]{:T(128)S(6)} %select_n.48), kind=kOutput, calls=%fused_computation.16 | convolution fusion | flops 1879048192 | bytes 7602180 | tf_op jit(solution)/shard_map/dot_general | solution.py:149
  198.6 0.0 copy-done.2
  198.6 3.7 %fusion.4 = f32[896,1024]{1,0:T(8,128)S(1)} fusion(bf16[896,1024]{1,0:T(8,128)(2,1)S(1)} %copy-done.2, bf16[4096,1024]{1,0:T(8,128)(2,1)} %bitcast.21, s32[]{:T(128)S(6)} %select_n.51), kind=kOutput, calls=%fused_computation.10 | convolution fusion | flops 1879048192 | bytes 7602180 | tf_op jit(solution)/shard_map/dot_general | solution.py:149
  202.4 27.2 %collective-permute-done.1 = bf16[896,1024]{1,0:T(8,128)(2,1)S(1)} collective-permute-done((bf16[896,1024]{1,0:T(8,128)(2,1)}, bf16[896,1024]{1,0:T(8,128)(2,1)S(1)}, u32[]{:S(2)}, u32[]{:S(2)}) %collective-permute-start.1) | collective-permute-done | bytes 1835040 | tf_op jit(solution)/shard_map/ppermute | solution.py:509
  229.5 1.9 add_convert_fusion.3
  231.5 2.1 collective-permute-start.2
  233.6 4.1 %collective-permute-done.4 = bf16[896,1024]{1,0:T(8,128)(2,1)} collective-permute-done((bf16[896,1024]{1,0:T(8,128)(2,1)}, bf16[896,1024]{1,0:T(8,128)(2,1)}, u32[]{:S(2)}, u32[]{:S(2)}) %collective-permute-start.4) | collective-permute-done | bytes 1835040 | tf_op jit(solution)/shard_map/ppermute | solution.py:509
  237.6 2.2 add_convert_fusion.1
  239.8 1.9 collective-permute-start.5
  241.8 4.2 %fusion.12 = f32[896,1024]{1,0:T(8,128)S(1)} fusion(bf16[896,1024]{1,0:T(8,128)(2,1)} %shard_map.120, bf16[4096,1024]{1,0:T(8,128)(2,1)} %bitcast.22, s32[]{:T(128)S(6)} %select_n.47), kind=kOutput, calls=%fused_computation.18 | convolution fusion | flops 1879048192 | bytes 7602180 | tf_op jit(solution)/shard_map/dot_general | solution.py:149
  246.0 30.2 %collective-permute-done.2 = bf16[896,1024]{1,0:T(8,128)(2,1)} collective-permute-done((bf16[896,1024]{1,0:T(8,128)(2,1)}, bf16[896,1024]{1,0:T(8,128)(2,1)}, u32[]{:S(2)}, u32[]{:S(2)}) %collective-permute-start.2) | collective-permute-done | bytes 1835040 | tf_op jit(solution)/shard_map/ppermute | solution.py:509
  276.3 7.9 %collective-permute-done.5 = bf16[896,1024]{1,0:T(8,128)(2,1)} collective-permute-done((bf16[896,1024]{1,0:T(8,128)(2,1)S(1)}, bf16[896,1024]{1,0:T(8,128)(2,1)}, u32[]{:S(2)}, u32[]{:S(2)}) %collective-permute-start.5) | collective-permute-done | bytes 1835040 | tf_op jit(solution)/shard_map/ppermute | solution.py:509
  284.2 4.4 %add_convert_fusion = bf16[896,1024]{1,0:T(8,128)(2,1)} fusion(bf16[896,1024]{1,0:T(8,128)(2,1)} %collective-permute-done.5, f32[896,1024]{1,0:T(8,128)S(1)} %fusion.12, bf16[896,1024]{1,0:T(8,128)(2,1)} %collective-permute-done.2), kind=kLoop, calls=%fused_computation.1 | loop fusion | flops 4587520 | bytes 9175040 | tf_op jit(solution)/shard_map/convert_element_type | solution.py:511
  288.6 1.3 fusion.34
  289.9 1.0 copy.15
  290.9 1.0 copy.16
  291.9 0.0 copy-done.4
  291.9 0.7 copy.19
  292.6 0.0 copy-done.3
  292.6 0.7 copy.20
  (5 shorter events, 0.0 us)
Async XLA Ops:
  7.2 281.4 %reduce-scatter.2.cloned.1.call-start = ((), (), s32[]{:S(2)}) async-start(), calls=%async_computation.1 | async-start | bytes 9437184 | tf_op jit(solution)/shard_map/reduce_scatter | solution.py:541
  129.2 1.5 copy-start
  135.7 43.7 %collective-permute-start = (bf16[896,1024]{1,0:T(8,128)(2,1)}, bf16[896,1024]{1,0:T(8,128)(2,1)}, u32[]{:S(2)}, u32[]{:S(2)}) collective-permute-start(bf16[896,1024]{1,0:T(8,128)(2,1)} %fusion.14), channel_id=1, source_target_pairs={{0,1},{4,5},{8,9},{12,13},{16,17},{20,21},{24,25},{28,29}} | collective-permute-start | bytes 5505032 | tf_op jit(solution)/shard_map/ppermute | solution.py:509
  142.2 44.7 %collective-permute-start.3 = (bf16[896,1024]{1,0:T(8,128)(2,1)}, bf16[896,1024]{1,0:T(8,128)(2,1)}, u32[]{:S(2)}, u32[]{:S(2)}) collective-permute-start(bf16[896,1024]{1,0:T(8,128)(2,1)} %fusion.17), channel_id=1, source_target_pairs={{3,2},{7,6},{11,10},{15,14},{19,18},{23,22},{27,26},{31,30}} | collective-permute-start | bytes 5505032 | tf_op jit(solution)/shard_map/ppermute | solution.py:509
  144.1 42.8 %copy-start.1 = (bf16[896,1024]{1,0:T(8,128)(2,1)S(1)}, bf16[896,1024]{1,0:T(8,128)(2,1)}, u32[]{:S(2)}) copy-start(bf16[896,1024]{1,0:T(8,128)(2,1)} %shard_map.120) | copy-start | bytes 5505028
  185.0 44.5 %collective-permute-start.1 = (bf16[896,1024]{1,0:T(8,128)(2,1)}, bf16[896,1024]{1,0:T(8,128)(2,1)S(1)}, u32[]{:S(2)}, u32[]{:S(2)}) collective-permute-start(bf16[896,1024]{1,0:T(8,128)(2,1)} %add_convert_fusion.4), channel_id=1, source_target_pairs={{0,1},{1,2},{4,5},{5,6},{8,9},{9,10},{12,13},{13,14},{16,17},{17,1... | collective-permute-start | bytes 5505032 | tf_op jit(solution)/shard_map/ppermute | solution.py:509
  192.9 44.7 %collective-permute-start.4 = (bf16[896,1024]{1,0:T(8,128)(2,1)}, bf16[896,1024]{1,0:T(8,128)(2,1)}, u32[]{:S(2)}, u32[]{:S(2)}) collective-permute-start(bf16[896,1024]{1,0:T(8,128)(2,1)} %add_convert_fusion.2), channel_id=1, source_target_pairs={{2,1},{3,2},{6,5},{7,6},{10,9},{11,10},{14,13},{15,14},{18,17},{19... | collective-permute-start | bytes 5505032 | tf_op jit(solution)/shard_map/ppermute | solution.py:509
  194.2 4.4 %copy-start.2 = (bf16[896,1024]{1,0:T(8,128)(2,1)S(1)}, bf16[896,1024]{1,0:T(8,128)(2,1)}, u32[]{:S(2)}) copy-start(bf16[896,1024]{1,0:T(8,128)(2,1)} %shard_map.120) | copy-start | bytes 5505028
  231.5 44.8 %collective-permute-start.2 = (bf16[896,1024]{1,0:T(8,128)(2,1)}, bf16[896,1024]{1,0:T(8,128)(2,1)}, u32[]{:S(2)}, u32[]{:S(2)}) collective-permute-start(bf16[896,1024]{1,0:T(8,128)(2,1)} %add_convert_fusion.3), channel_id=1, source_target_pairs={{0,1},{1,2},{2,3},{4,5},{5,6},{6,7},{8,9},{9,10},{10,11},{12,13},{... | collective-permute-start | bytes 5505032 | tf_op jit(solution)/shard_map/ppermute | solution.py:509
  239.8 44.4 %collective-permute-start.5 = (bf16[896,1024]{1,0:T(8,128)(2,1)S(1)}, bf16[896,1024]{1,0:T(8,128)(2,1)}, u32[]{:S(2)}, u32[]{:S(2)}) collective-permute-start(bf16[896,1024]{1,0:T(8,128)(2,1)S(1)} %add_convert_fusion.1), channel_id=1, source_target_pairs={{1,0},{2,1},{3,2},{5,4},{6,5},{7,6},{9,8},{10,9},{11,10},{13,12},{... | collective-permute-start | bytes 5505032 | tf_op jit(solution)/shard_map/ppermute | solution.py:509
  288.6 3.3 %copy-start.4 = (bf16[256,512]{1,0:T(8,128)(2,1)S(1)}, bf16[256,512]{1,0:T(8,128)(2,1)}, u32[]{:S(2)}) copy-start(bf16[256,512]{1,0:T(8,128)(2,1)} %get-tuple-element.34) | copy-start | bytes 786436
  288.6 4.0 %copy-start.3 = (bf16[256,512]{1,0:T(8,128)(2,1)S(1)}, bf16[256,512]{1,0:T(8,128)(2,1)}, u32[]{:S(2)}) copy-start(bf16[256,512]{1,0:T(8,128)(2,1)} %get-tuple-element.35) | copy-start | bytes 786436
Sparse Core Ops, SparseCore 0:
  129.4 73.6 reduce-scatter.1

commit v2 on v1

--- a/solution.py
+++ b/solution.py
@@ -491,24 +491,126 @@
     )
 
 
-def line_sum(part_of, count):
+def line_kernel(
+    count, own_ref, weights_hbm, out_ref, weights, got, sent, total, load_sem, send_sem, recv_sem
+):
     z = lax.axis_index("mp")
-    total = part_of(z)
-    for direction in (1, -1):
-        carried = None
-        for step in range(count - 1):
-            if direction == 1:
-                dest = jnp.clip(z + count - 1 - step, 0, count - 1)
-                pairs = [(k, k + 1) for k in range(count - 1) if k <= step]
-            else:
-                dest = jnp.clip(z - (count - 1) + step, 0, count - 1)
-                pairs = [(k, k - 1) for k in range(1, count) if count - 1 - k <= step]
-            term = part_of(dest)
-            if carried is not None:
-                term = term + carried.astype(jnp.float32)
-            carried = lax.ppermute(term.astype(jnp.bfloat16), "mp", pairs)
-        total = total + carried.astype(jnp.float32)
-    return total.astype(jnp.bfloat16)
+    chunks = own_ref.shape[0] // BLK
+    right, left = (z + 1) % count, (z + count - 1) % count
+    loads = [
+        pltpu.make_async_copy(weights_hbm.at[d], weights.at[d], load_sem.at[d])
+        for d in range(count)
+    ]
+    for load in loads:
+        load.start()
+    barrier = pltpu.get_barrier_semaphore()
+    for d in range(1, count):
+        pl.semaphore_signal(
+            barrier, inc=1, device_id={"mp": (z + d) % count}, device_id_type=MESH
+        )
+    pl.semaphore_wait(barrier, count - 1)
+    for load in loads:
+        load.wait()
+
+    def link(way, dest, r):
+        return pltpu.make_async_remote_copy(
+            src_ref=sent.at[way, dest, r],
+            dst_ref=got.at[way, dest, r],
+            send_sem=send_sem.at[way, dest, r],
+            recv_sem=recv_sem.at[way, dest, r],
+            device_id={"mp": left if way else right},
+            device_id_type=MESH,
+        )
+
+    def rows(r):
+        return pl.ds(pl.multiple_of(r * BLK, BLK), BLK)
+
+    def pass_on(way, dest, r):
+        first = z == (count - 1 if way else 0)
+        total[...] = contract(own_ref[rows(r), :], weights[dest], 1, 1)
+
+        @pl.when(first)
+        def _():
+            sent[way, dest, r] = total[...].astype(jnp.bfloat16)
+
+        @pl.when(jnp.logical_not(first))
+        def _():
+            link(way, dest, r).wait_recv()
+            added = total[...] + got[way, dest, r].astype(jnp.float32)
+            sent[way, dest, r] = added.astype(jnp.bfloat16)
+
+        link(way, dest, r).start()
+
+    for phase in range(count - 1):
+
+        @pl.loop(0, chunks)
+        def _(r):
+            @pl.when(z < count - 1 - phase)
+            def _():
+                pass_on(0, count - 1 - phase, r)
+
+            @pl.when(z > phase)
+            def _():
+                pass_on(1, phase, r)
+
+    @pl.loop(0, chunks)
+    def _(r):
+        total[...] = contract(own_ref[rows(r), :], weights[z], 1, 1)
+
+        @pl.when(z > 0)
+        def _():
+            link(0, z, r).wait_recv()
+            total[...] += got[0, z, r].astype(jnp.float32)
+
+        @pl.when(z < count - 1)
+        def _():
+            link(1, z, r).wait_recv()
+            total[...] += got[1, z, r].astype(jnp.float32)
+
+        out_ref[rows(r), :] = total[...].astype(jnp.bfloat16)
+
+    for phase in range(count - 1):
+
+        @pl.loop(0, chunks)
+        def _(r):
+            @pl.when(z < count - 1 - phase)
+            def _():
+                link(0, count - 1 - phase, r).wait_send()
+
+            @pl.when(z > phase)
+            def _():
+                link(1, phase, r).wait_send()
+
+
+def line_sum(own, weights, count):
+    rows, width = own.shape
+    out_width = weights.shape[0] // count
+    chunks = rows // BLK
+    vmem = pl.BlockSpec(memory_space=pltpu.VMEM)
+    dma = pltpu.SemaphoreType.DMA
+    return pl.pallas_call(
+        functools.partial(line_kernel, count),
+        out_shape=jax.ShapeDtypeStruct((rows, out_width), own.dtype),
+        in_specs=[vmem, pl.BlockSpec(memory_space=pl.ANY)],
+        out_specs=vmem,
+        scratch_shapes=[
+            pltpu.VMEM((count, out_width, width), own.dtype),
+            pltpu.VMEM((2, count, chunks, BLK, out_width), own.dtype),
+            pltpu.VMEM((2, count, chunks, BLK, out_width), own.dtype),
+            pltpu.VMEM((BLK, out_width), jnp.float32),
+            dma((count,)),
+            dma((2, count, chunks)),
+            dma((2, count, chunks)),
+        ],
+        compiler_params=pltpu.CompilerParams(
+            collective_id=1, has_side_effects=True, vmem_limit_bytes=58 * 1024 * 1024
+        ),
+        cost_estimate=pl.CostEstimate(
+            flops=2 * rows * width * out_width * count,
+            bytes_accessed=300 * 1024 * 1024,
+            transcendentals=0,
+        ),
+    )(own, weights.reshape(count, out_width, width))
 
 
 def per_device_cube(
@@ -536,17 +638,11 @@
     )
     weights = weights.reshape(-1, 2 * width)
     own = pick_blocks(back, block_bin)
-    out_width = weights.shape[0] // count
     weight_terms = contract(encoder_rows, own, 0, 0)
     weight_sums = lax.psum_scatter(
         weight_terms.astype(jnp.bfloat16), "dp", scatter_dimension=0, tiled=True
     )
-
-    def part_of(dest):
-        piece = lax.dynamic_slice_in_dim(weights, dest * out_width, out_width, 0)
-        return contract(own, piece, 1, 1)
-
-    encoder_grad = line_sum(part_of, count)
+    encoder_grad = line_sum(own, weights, count)
     return context, query_grad, encoder_grad, weight_sums[:, :width], weight_sums[:, width:]
 
 

time: 302 us -> 299 us (0.990)
  Pallas kernels: 99.4 us -> 254 us
  waiting for transfers between devices: 105 us -> 0.04 us
  matrix products: 47.8 us -> 13.8 us
  starting transfers between devices: 10.5 us -> 0.04 us
  other arithmetic: 11.2 us -> 2.73 us
    pallas_call x0 -> x1, Pallas kernels: none -> 154 us  [line_sum(): pl.pallas_call(functools.partial(line_kernel, count), out_shape=jax.Shape...]
    ppermute x6 -> x0, waiting for transfers between devices: 105 us -> none  [line_sum(): carried = lax.ppermute(term.astype(jnp.bfloat16), 'mp', pairs)]
    dot_general x8 -> x1, matrix products: 47.8 us -> 13.8 us  [contract(): lax.dot_general(a, b, (((dim_a,), (dim_b,)), ((), ())), preferred_element...]
    ppermute x6 -> x0, starting transfers between devices: 10.4 us -> none  [line_sum(): carried = lax.ppermute(term.astype(jnp.bfloat16), 'mp', pairs)]
    convert_element_type x3 -> x0, other arithmetic: 8.49 us -> none  [the longest x1 4.39 us: line_sum(): return total.astype(jnp.bfloat16)]
    unnamed x14 -> x9, local copies, waits for them, and re-layouts: 4.9 us -> 6.29 us
  transfers between devices with their start and end apart: 7 -> 1, of which waited for: 5 -> 0; matrix products, arithmetic and copies ran while one was open for 14% -> 0% of each run, Pallas kernels for 0% -> 52%
where the time goes in v2:
time: 299 us; the launch traced here: 298 us
  Pallas kernels  254 us (85%)
  between operations  16.7 us (6%)
  matrix products  13.8 us (5%)
  local copies, waits for them, and re-layouts  11.1 us (4%)
    pallas_call x1, Pallas kernels, line_sum(): pl.pallas_call(functools.partial(line_kernel, count), out_shape=jax.Shape...  154 us
    pallas_call x1, Pallas kernels, front(): pl.pallas_call(functools.partial(front_kernel, n), out_shape=(jax.ShapeDt...  93.6 us
    dot_general x1, matrix products, contract(): lax.dot_general(a, b, (((dim_a,), (dim_b,)), ((), ())), preferred_element...  13.8 us
    unnamed x9, local copies, waits for them, and re-layouts  6.29 us
  transfers between devices with their start and end apart: 1, of which 0 were waited for; matrix products, arithmetic and copies ran while one was open for 0% of the time, Pallas kernels for 52%

profile of v2, /device:TPU:10, one launch (start us, length us, event | category | flops | bytes accessed | tf_op | source)
XLA Modules:
  0.0 298.2 jit_solution(16317064060790212945)
XLA Ops:
  7.2 0.0 reduce-scatter.2.cloned.1.call-start
  7.2 0.7 broadcast_add_fusion
  7.9 0.7 iota_compare_fusion
  8.5 0.7 select_reduce_fusion
  9.3 1.4 fusion.4
  13.3 0.7 fusion.2
  13.9 0.7 broadcast_in_dim.44.routes_ref
  14.6 0.7 broadcast_in_dim.43.tags_ref
  15.3 0.8 iota.21.token_doc_ref
  16.1 93.6 %shard_map.119 = (bf16[256,512]{1,0:T(8,128)(2,1)}, bf16[256,512]{1,0:T(8,128)(2,1)}, bf16[2,2,1024,256]{3,2,1,0:T(8,128)(2,1)}, bf16[8,512,1024]{2,1,0:T(8,128)(2,1)}) custom-call(bf16[256,512]{1,0:T(8,128)(2,1)} %q_ref.1, bf16[256,512]{1,0:T(8,128)(2,1)} %g_ref.1, bf16[896,4096]{1,0:T(8,128)(2,1)} %enc_hbm.1, bf16[512,512]{1,0:T(8,128)(2,1)} %kw_ref.1, ...), custom_call_target="tpu_custom_call" | custom-call | tf_op jit(solution)/shard_map/pallas_call | solution.py:450
  109.7 5.8 %shard_map.120.own_ref = bf16[896,1024]{1,0:T(8,128)(2,1)} custom-call(s32[7]{0:T(128)} %bins_ref.1, bf16[2,2,1024,256]{3,2,1,0:T(8,128)(2,1)} %get-tuple-element.11.back_ref), custom_call_target="tpu_custom_call" | custom-call | tf_op jit(solution)/shard_map/pallas_call | solution.py:418
  115.5 13.8 %convert_bitcast_fusion = bf16[4096,1024]{0,1:T(8,128)(2,1)} fusion(bf16[896,1024]{1,0:T(8,128)(2,1)} %shard_map.120.own_ref, bf16[896,4096]{1,0:T(8,128)(2,1)} %enc_hbm.1), kind=kOutput, calls=%fused_computation | convolution fusion | flops 7520387072 | bytes 17563648 | tf_op jit(solution)/shard_map/dot_general | solution.py:149
  129.3 0.0 reduce-scatter.2.cloned.1.call-update
  129.3 0.0 copy-start.1
  129.3 0.0 copy-start
  129.3 154.4 %shard_map.121 = bf16[896,1024]{1,0:T(8,128)(2,1)} custom-call(bf16[896,1024]{1,0:T(8,128)(2,1)} %shard_map.120.own_ref, bf16[4,1024,1024]{2,1,0:T(8,128)(2,1)} %bitcast.9), custom_call_target="tpu_custom_call" | custom-call | flops 7516192768 | bytes 314572800 | tf_op jit(solution)/shard_map/pallas_call | solution.py:591
  283.8 0.0 reduce-scatter.2.cloned.1.call-done
  283.8 1.3 fusion.3
  285.1 1.0 copy.16
  286.1 1.0 copy.15
  287.1 0.0 copy-done.1
  287.1 0.7 copy.20
  287.8 0.0 copy-done
  287.8 0.7 copy.21
  288.5 2.9 copy.22
  (2 shorter events, 0.0 us)
Async XLA Ops:
  7.2 276.6 %reduce-scatter.2.cloned.1.call-start = ((), (), s32[]{:S(2)}) async-start(), calls=%async_computation.1 | async-start | bytes 9437184 | tf_op jit(solution)/shard_map/reduce_scatter | solution.py:642
  129.3 157.8 %copy-start.1 = (bf16[256,512]{1,0:T(8,128)(2,1)S(1)}, bf16[256,512]{1,0:T(8,128)(2,1)}, u32[]{:S(2)}) copy-start(bf16[256,512]{1,0:T(8,128)(2,1)} %get-tuple-element.34) | copy-start | bytes 786436
  129.3 158.5 %copy-start = (bf16[256,512]{1,0:T(8,128)(2,1)S(1)}, bf16[256,512]{1,0:T(8,128)(2,1)}, u32[]{:S(2)}) copy-start(bf16[256,512]{1,0:T(8,128)(2,1)} %get-tuple-element.35) | copy-start | bytes 786436
Sparse Core Ops, SparseCore 0:
  129.4 73.6 reduce-scatter.1
